TPU v7x, 32 devices: a whole 2x2x4 slice. The times are simulated.
32 devices in a mesh: img: 4 (over z), seq: 4 (over x, core), head: 2 (over y).
Axes of the slice: x: 2, y: 2, z: 4, core: 2. Of those that a mesh axis runs over, the one named last changes fastest.
Arguments:
- self_qkv: bfloat16 [4, 1024, 3072], P('img', ('seq', 'head')), may hold values from -12 to 12
- cross_query: bfloat16 [4, 1024, 1024], P('img', ('seq', 'head')), may hold values from -12 to 12
- thermal_kv: bfloat16 [4, 8, 256, 2048], P('img', ('seq', 'head')), may hold values from -12 to 12
- owners: int32 [4], P('img'), may hold values from 0 to 7
- grad_out: bfloat16 [4, 1024, 1024], P('img', ('seq', 'head')), may hold values from -6 to 6
Outputs:
- combined: bfloat16 [4, 1024, 1024], P('img', ('seq', 'head'))
- grad_qkv: bfloat16 [4, 1024, 3072], P('img', ('seq', 'head'))
- grad_cross_query: bfloat16 [4, 1024, 1024], P('img', ('seq', 'head'))
- grad_thermal: bfloat16 [4, 256, 2048], P('img', ('seq', 'head'))
All inputs are finite; a program needn't handle non-finite values.
Results may differ from a plain program's by a relative error of at most 0.012.
The roundings to bfloat16 on the way count: a program that leaves them out, or rounds other values in their place, can miss the bound.
Values may be sent and summed in bfloat16 or wider, within the bound.
No kernel may reach another device: no remote copies, remote signals or barrier semaphores. Data moves between devices by JAX's collectives and lax.ppermute only.
A program may use at most 128 MiB of HBM per device.

v0:
```python
import math
import jax
import jax.numpy as jnp
from jax import lax
from jax.sharding import PartitionSpec as P

HEADS = 16
HD = 64


def spread(block, axis, owner):
    block = jnp.where(lax.axis_index(axis) == owner, block, jnp.zeros_like(block))
    return lax.psum(block, axis)


def log_total(scores):
    row_max = jnp.max(scores, axis=-1, keepdims=True)
    return row_max + jnp.log(jnp.sum(jnp.exp(scores - row_max), axis=-1, keepdims=True))


def output_delta(upstream, mixed):
    return jnp.sum(upstream.astype(jnp.float32) * mixed, axis=-1).T[:, :, None]


def cross_block(cross_heads, upstream, thermal_keys, thermal_values, score_scale):
    cross_scores = (
        jnp.einsum("qhd,khd->hqk", cross_heads, thermal_keys, preferred_element_type=jnp.float32)
        * score_scale
    )
    cross_lse = log_total(cross_scores)
    cross_probs = jnp.exp(cross_scores - cross_lse).astype(jnp.bfloat16)
    cross_mixed = jnp.einsum(
        "hqk,khd->qhd", cross_probs, thermal_values, preferred_element_type=jnp.float32
    )
    cross_dprobs = jnp.einsum(
        "qhd,khd->hqk", upstream, thermal_values, preferred_element_type=jnp.float32
    )
    cross_delta = output_delta(upstream, cross_mixed)
    cross_dscores = (
        cross_probs.astype(jnp.float32) * (cross_dprobs - cross_delta) * score_scale
    ).astype(jnp.bfloat16)
    cross_dq = jnp.einsum(
        "hqk,khd->qhd", cross_dscores, thermal_keys, preferred_element_type=jnp.float32
    )
    return (cross_mixed, cross_probs, cross_dscores, cross_dq)


def thermal_sums(cross_probs, cross_dscores, cross_heads, upstream, row_span):
    key_grad = jnp.einsum(
        "hqk,qhd->khd", cross_dscores, cross_heads, preferred_element_type=jnp.float32
    )
    value_grad = jnp.einsum(
        "hqk,qhd->khd", cross_probs, upstream, preferred_element_type=jnp.float32
    )
    width = key_grad.shape[1] * key_grad.shape[2]
    return jnp.concatenate(
        [key_grad.reshape(row_span, width), value_grad.reshape(row_span, width)], axis=1
    )


def body(self_qkv, cross_query, thermal_kv, owners, grad_out):
    tokens_here = self_qkv.shape[1]
    model_width = cross_query.shape[2]
    head_devices = lax.axis_size("head")
    heads_local = HEADS // head_devices
    local_width = heads_local * HD
    score_scale = 1.0 / math.sqrt(HD)
    thermal_rows = thermal_kv.shape[2]
    packed = self_qkv[0].reshape(tokens_here, 3, head_devices, local_width)
    by_heads = lax.all_to_all(packed, "head", split_axis=2, concat_axis=0, tiled=True)
    row_count = by_heads.shape[0]
    query_flat = by_heads[:, 0, 0]
    keys_all, values_all = (
        lax.all_gather(by_heads[:, 1, 0], "seq", axis=0, tiled=True),
        lax.all_gather(by_heads[:, 2, 0], "seq", axis=0, tiled=True),
    )
    key_rows = keys_all.shape[0]
    query_here = query_flat.reshape(row_count, heads_local, HD)
    keys_heads = keys_all.reshape(key_rows, heads_local, HD)
    values_heads = values_all.reshape(key_rows, heads_local, HD)
    scores = (
        jnp.einsum("qhd,khd->hqk", query_here, keys_heads, preferred_element_type=jnp.float32)
        * score_scale
    )
    self_lse = log_total(scores)
    self_probs = jnp.exp(scores - self_lse).astype(jnp.bfloat16)
    attended_wide = jnp.einsum(
        "hqk,khd->qhd", self_probs, values_heads, preferred_element_type=jnp.float32
    )
    attended_heads = attended_wide.astype(jnp.bfloat16)
    attended = lax.all_to_all(
        attended_heads.reshape(row_count, 1, local_width),
        "head",
        split_axis=0,
        concat_axis=1,
        tiled=True,
    )
    attended = attended.reshape(tokens_here, model_width)
    thermal = spread(thermal_kv[0, 0], ("seq", "head"), owners[0])
    cross_in = (attended.astype(jnp.float32) + cross_query[0].astype(jnp.float32)).astype(
        jnp.bfloat16
    )
    cross_heads = cross_in.reshape(tokens_here, HEADS, HD)
    upstream = grad_out[0].reshape(tokens_here, HEADS, HD)
    thermal_keys = thermal[:, :model_width].reshape(thermal_rows, HEADS, HD)
    thermal_values = thermal[:, model_width:].reshape(thermal_rows, HEADS, HD)
    cross_mixed, cross_probs, cross_dscores, cross_dq = cross_block(
        cross_heads, upstream, thermal_keys, thermal_values, score_scale
    )
    combined = (
        attended.astype(jnp.float32) + cross_mixed.reshape(tokens_here, model_width)
    ).astype(jnp.bfloat16)
    cross_dq = cross_dq.reshape(tokens_here, model_width)
    group_devices = lax.axis_size("seq") * head_devices
    grad_thermal = lax.psum_scatter(
        thermal_sums(
            cross_probs,
            cross_dscores,
            cross_heads,
            upstream,
            lax.axis_size(("seq", "head")) * (thermal_rows // group_devices),
        ),
        ("seq", "head"),
        scatter_dimension=0,
        tiled=True,
    ).astype(jnp.bfloat16)
    grad_cross = cross_dq.astype(jnp.bfloat16)
    attended_grad = (grad_out[0].astype(jnp.float32) + cross_dq).astype(jnp.bfloat16)
    grad_heads = lax.all_to_all(
        attended_grad.reshape(tokens_here, head_devices, local_width),
        "head",
        split_axis=1,
        concat_axis=0,
        tiled=True,
    )
    grad_flat = grad_heads.reshape(row_count, local_width)
    grad_here = grad_flat.reshape(row_count, heads_local, HD)
    self_dprobs = jnp.einsum(
        "qhd,khd->hqk", grad_here, values_heads, preferred_element_type=jnp.float32
    )
    self_delta = output_delta(grad_here, attended_wide)
    self_dscores = (
        self_probs.astype(jnp.float32) * (self_dprobs - self_delta) * score_scale
    ).astype(jnp.bfloat16)
    query_grad = jnp.einsum(
        "hqk,khd->qhd", self_dscores, keys_heads, preferred_element_type=jnp.float32
    )
    query_grad = query_grad.reshape(row_count, local_width)
    key_grad = jnp.einsum(
        "hqk,qhd->khd", self_dscores, query_here, preferred_element_type=jnp.float32
    )
    value_grad = jnp.einsum(
        "hqk,qhd->khd", self_probs, grad_here, preferred_element_type=jnp.float32
    )
    own_grads = lax.psum_scatter(
        jnp.concatenate(
            [
                key_grad.reshape(lax.axis_size("seq") * row_count, local_width),
                value_grad.reshape(lax.axis_size("seq") * row_count, local_width),
            ],
            axis=1,
        ),
        "seq",
        scatter_dimension=0,
        tiled=True,
    )
    key_own = own_grads[:, :local_width]
    value_own = own_grads[:, local_width:]
    stacked = jnp.stack([query_grad, key_own, value_own], axis=1).astype(jnp.bfloat16)
    stacked = stacked.reshape(row_count, 3, 1, local_width)
    grad_qkv = lax.all_to_all(stacked, "head", split_axis=0, concat_axis=2, tiled=True).reshape(
        tokens_here, 3 * model_width
    )
    return (combined[None], grad_qkv[None], grad_cross[None], grad_thermal[None])


def solution(mesh):
    placed = (
        P("img", ("seq", "head"), None),
        P("img", ("seq", "head"), None),
        P("img", ("seq", "head"), None, None),
        P("img"),
        P("img", ("seq", "head"), None),
    )
    return jax.shard_map(
        body,
        mesh=mesh,
        in_specs=placed,
        out_specs=(
            P("img", ("seq", "head"), None),
            P("img", ("seq", "head"), None),
            P("img", ("seq", "head"), None),
            P("img", ("seq", "head"), None),
        ),
        check_vma=False,
    )
```

profile of v0, /device:TPU:0, one launch (start us, length us, event | category | flops | bytes accessed | tf_op | source)
XLA Modules:
  0.0 235.7 jit_solution(8329508114149124383)
XLA Ops:
  8.1 1.6 copy.134
  9.9 14.9 %all_to_all.57 = bf16[128,3,2,512]{3,0,1,2:T(8,128)(2,1)S(1)} all-to-all(bf16[128,3,2,512]{3,0,1,2:T(8,128)(2,1)S(1)} %copy.135), channel_id=1, replica_groups=mesh['img'=4,'seq'=4,'head'=2] {'head'}, dimensions={2} | all-to-all | bytes 1572864 | tf_op jit(solution)/shard_map/all_to_all | solution.py:70
  25.0 0.8 fusion.9
  27.3 1.1 select_bitcast_fusion
  28.6 0.9 copy.147
  29.9 13.5 %all-gather.5.cloned.1.call-done = bf16[1024,1,1,512]{3,0,1,2:T(8,128)(2,1)} async-done(((bf16[256,1,1,512]{3,0,1,2:T(8,128)(2,1)}), bf16[1024,1,1,512]{3,0,1,2:T(8,128)(2,1)}) %all-gather.5.cloned.1.call-update) | async-done | bytes 1048592 | tf_op jit(solution)/shard_map/all_gather | solution.py:74
  43.4 1.5 copy.138
  44.9 1.4 multiply_reduce_fusion
  46.3 1.7 exponential_reduce_fusion
  48.0 2.7 %exponential_convert_fusion = bf16[8,256,1024]{2,1,0:T(8,128)(2,1)} fusion(f32[8,256,1024]{2,1,0:T(8,128)S(1)} %get-tuple-element.40, f32[8,256]{1,0:T(8,128)S(1)} %log_add_fusion.1), kind=kLoop, calls=%fused_computation.1 | loop fusion | flops 6291456 | bytes 12591104 | tf_op jit(solution)/shard_map/convert_element_type | solution.py:86
  50.7 11.8 %all-gather.7.cloned.1.call-done = bf16[1024,1,1,512]{3,0,1,2:T(8,128)(2,1)} async-done(((bf16[256,1,1,512]{3,0,1,2:T(8,128)(2,1)}), bf16[1024,1,1,512]{3,0,1,2:T(8,128)(2,1)}) %all-gather.7.cloned.1.call-update) | async-done | bytes 1048592 | tf_op jit(solution)/shard_map/all_gather | solution.py:75
  62.5 1.5 copy.139
  64.0 4.8 %fusion.10 = (bf16[256,8,64]{0,2,1:T(8,128)(2,1)S(1)}, f32[256,8,64]{0,2,1:T(8,128)}) fusion(bf16[8,256,1024]{2,1,0:T(8,128)(2,1)} %exponential_convert_fusion, bf16[1024,8,64]{0,2,1:T(8,128)(2,1)S(1)} %bitcast.102), kind=kOutput, calls=%fused_computation.33 | convolution fusion | flops 268566528 | bytes 6029312 | tf_op jit(solution)/shard_map/hqk,khd->qhd/dot_general | solution.py:87
  69.3 0.8 reduce
  70.2 0.9 reshape.190
  71.1 3.4 %all-to-all-start.1 = ((bf16[2,2,32768]{2,1,0:T(2,128)(2,1)}), bf16[2,2,32768]{2,1,0:T(2,128)(2,1)S(1)}, u32[]{:S(2)}, u32[]{:S(2)}) async-start(bf16[2,2,32768]{2,1,0:T(2,128)(2,1)} %reshape.190), calls=%async_computation.1 | async-start | bytes 524288 | tf_op jit(solution)/shard_map/all_to_all | solution.py:91
  74.6 18.7 %all-reduce.2.cloned.1.call-done = bf16[256,2048]{1,0:T(8,128)(2,1)} async-done(((bf16[256,2048]{1,0:T(8,128)(2,1)}), bf16[256,2048]{1,0:T(8,128)(2,1)}) %all-reduce.2.cloned.1.call-update) | async-done | bytes 1048592 | tf_op jit(solution)/shard_map/psum | solution.py:13
  93.3 2.1 fusion.8
  95.6 1.4 copy.143
  97.1 1.0 reshape.191
  98.0 1.3 copy.141
  101.2 1.3 fusion.3
  102.5 1.6 fusion.1
  104.1 1.2 bitcast_convert_fusion
  105.4 7.6 %all_to_all.58 = bf16[128,2,512]{0,2,1:T(8,128)(2,1)S(1)} all-to-all(bf16[128,2,512]{0,2,1:T(8,128)(2,1)S(1)} %add_convert_fusion), channel_id=1, replica_groups=mesh['img'=4,'seq'=4,'head'=2] {'head'}, dimensions={1} | all-to-all | bytes 524288 | tf_op jit(solution)/shard_map/all_to_all | solution.py:129
  112.9 1.0 copy.150
  113.9 1.1 reshape_reshape.3
  115.1 4.5 %fusion.11 = f32[8,64,1024]{2,1,0:T(8,128)} fusion(bf16[256,8,64]{0,2,1:T(8,128)(2,1)S(1)} %reshape_reshape.3, bf16[8,256,1024]{2,1,0:T(8,128)(2,1)} %exponential_convert_fusion), kind=kOutput, calls=%fused_computation.34 | convolution fusion | flops 268435456 | bytes 6553600 | tf_op jit(solution)/shard_map/hqk,qhd->khd/dot_general | solution.py:152
  119.7 1.9 multiply_convert_fusion
  121.7 1.9 copy-done.1
  123.6 2.2 fusion.12
  125.8 3.0 %copy.151 = f32[1024,512]{1,0:T(8,128)} copy(f32[1024,512]{0,1:T(8,128)} %bitcast.105) | data formatting | bytes 4194304 | tf_op jit(solution)/shard_map/reshape | solution.py:158
  128.8 2.9 %copy.152 = f32[1024,512]{1,0:T(8,128)} copy(f32[1024,512]{0,1:T(8,128)} %bitcast.104) | data formatting | bytes 4194304 | tf_op jit(solution)/shard_map/reshape | solution.py:159
  131.7 4.7 %pad_maximum_fusion = f32[1024,1024]{1,0:T(8,128)} fusion(f32[1024,512]{1,0:T(8,128)} %copy.152, f32[1024,512]{1,0:T(8,128)} %copy.151), kind=kLoop, calls=%fused_computation.4 | loop fusion | flops 1048576 | bytes 8388608 | tf_op jit(solution)/shard_map/concatenate | solution.py:156
  136.5 2.5 %fusion.4 = f32[16,64,256]{2,1,0:T(8,128)} fusion(bf16[16,128,256]{2,1,0:T(8,128)(2,1)S(1)} %fusion.1, f32[128,16,64]{0,2,1:T(8,128)} %bitcast.107, bf16[128,16,64]{0,2,1:T(8,128)(2,1)} %bitcast.125), kind=kOutput, calls=%fused_computation.29 | convolution fusion | flops 67502080 | bytes 2883584 | tf_op jit(solution)/shard_map/hqk,qhd->khd/dot_general | solution.py:49
  139.0 2.6 %copy.157 = f32[256,1024]{1,0:T(8,128)} copy(f32[256,1024]{0,1:T(8,128)} %bitcast.117) | data formatting | bytes 2097152 | tf_op jit(solution)/shard_map/reshape | solution.py:57
  141.8 1.4 copy.158
  143.2 3.8 %pad_maximum_fusion.1 = f32[256,2048]{1,0:T(8,128)} fusion(f32[256,1024]{1,0:T(8,128)} %copy.158, f32[256,1024]{1,0:T(8,128)} %copy.157), kind=kLoop, calls=%fused_computation.5 | loop fusion | flops 524288 | bytes 4194304 | tf_op jit(solution)/shard_map/concatenate | solution.py:56
  147.1 0.9 copy.160
  148.3 0.8 add_convert_fusion.1
  149.1 3.6 %convolution_convert_fusion = bf16[8,256,64]{1,2,0:T(8,128)(2,1)S(1)} fusion(bf16[8,256,1024]{2,1,0:T(8,128)(2,1)} %copy-done.1, bf16[1024,8,64]{0,2,1:T(8,128)(2,1)S(1)} %bitcast.101), kind=kOutput, calls=%fused_computation.13 | convolution fusion | flops 268566528 | bytes 5505024 | tf_op jit(solution)/shard_map/hqk,khd->qhd/dot_general | solution.py:145
  152.8 27.6 %reduce-scatter.3.cloned.1.call-done = f32[256,1024]{1,0:T(8,128)} async-done(((f32[1024,1024]{1,0:T(8,128)}), f32[256,1024]{1,0:T(8,128)}) %reduce-scatter.3.cloned.1.call-update) | async-done | bytes 1048592 | tf_op jit(solution)/shard_map/reduce_scatter | solution.py:155
  180.4 1.3 convert.22
  181.9 1.7 copy.154
  183.5 3.6 %all-to-all-start.3 = ((bf16[256,3,1,512]{3,1,2,0:T(4,128)(2,1)}), bf16[256,3,1,512]{3,1,2,0:T(4,128)(2,1)S(1)}, u32[]{:S(2)}, u32[]{:S(2)}) async-start(bf16[256,3,1,512]{3,1,2,0:T(4,128)(2,1)} %copy.154), calls=%async_computation.4 | async-start | bytes 2097152 | tf_op jit(solution)/shard_map/all_to_all | solution.py:171
  187.1 38.1 %reduce-scatter.5.cloned.1.call-done = f32[32,2048]{1,0:T(8,128)} async-done(((f32[256,2048]{1,0:T(8,128)}), f32[32,2048]{1,0:T(8,128)}) %reduce-scatter.5.cloned.1.call-update) | async-done | bytes 262160 | tf_op jit(solution)/shard_map/reduce_scatter | solution.py:115
  225.2 1.6 convert_bitcast_fusion
  227.4 1.2 copy.159
  (76 shorter events, 6.1 us)
Async XLA Ops:
  8.0 19.3 %copy-start.17 = (bf16[1,1,256,2048]{3,2,1,0:T(8,128)(2,1)S(1)}, bf16[1,1,256,2048]{3,2,1,0:T(8,128)(2,1)}, u32[]{:S(2)}) copy-start(bf16[1,1,256,2048]{3,2,1,0:T(8,128)(2,1)} %param.7) | copy-start | bytes 3145732
  8.0 35.4 %all-gather.5.cloned.1.call-start = ((), (), s32[]{:S(2)}) async-start(), calls=%async_computation.9 | async-start | bytes 1310720 | tf_op jit(solution)/shard_map/all_gather | solution.py:74
  9.9 18.5 %copy-start.18 = (bf16[1,128,1024]{2,1,0:T(8,128)(2,1)S(1)}, bf16[1,128,1024]{2,1,0:T(8,128)(2,1)}, u32[]{:S(2)}) copy-start(bf16[1,128,1024]{2,1,0:T(8,128)(2,1)} %param.9) | copy-start | bytes 786436
  24.9 4.7 %copy-start.20 = (bf16[1,128,1024]{2,1,0:T(8,128)(2,1)S(1)}, bf16[1,128,1024]{2,1,0:T(8,128)(2,1)}, u32[]{:S(2)}) copy-start(bf16[1,128,1024]{2,1,0:T(8,128)(2,1)} %param.6) | copy-start | bytes 786436
  25.8 36.6 %all-gather.7.cloned.1.call-start = ((), (), s32[]{:S(2)}) async-start(), calls=%async_computation.10 | async-start | bytes 1310720 | tf_op jit(solution)/shard_map/all_gather | solution.py:75
  26.6 66.7 %all-reduce.2.cloned.1.call-start = ((), (), s32[]{:S(2)}) async-start(), calls=%async_computation.6 | async-start | bytes 2097152 | tf_op jit(solution)/shard_map/psum | solution.py:13
  28.6 73.9 %copy-start.9 = (bf16[1,128,1024]{1,2,0:T(8,128)(2,1)}, bf16[1,128,1024]{1,2,0:T(8,128)(2,1)S(1)}, u32[]{:S(2)}) copy-start(bf16[1,128,1024]{1,2,0:T(8,128)(2,1)S(1)} %copy.148) | copy-start | bytes 786436
  29.7 69.6 %copy-start.13 = (bf16[1,128,1024]{1,2,0:T(8,128)(2,1)}, bf16[1,128,1024]{1,2,0:T(8,128)(2,1)S(1)}, u32[]{:S(2)}) copy-start(bf16[1,128,1024]{1,2,0:T(8,128)(2,1)S(1)} %copy.144) | copy-start | bytes 786436
  29.9 16.4 %copy-start.11 = (bf16[256,1,1,512]{0,3,2,1:T(8,128)(2,1)}, bf16[256,1,1,512]{0,3,2,1:T(8,128)(2,1)S(1)}, u32[]{:S(2)}) copy-start(bf16[256,1,1,512]{0,3,2,1:T(8,128)(2,1)S(1)} %copy.137) | copy-start | bytes 786436
  64.0 31.4 %copy-start.2 = (bf16[1024,1,1,512]{0,3,2,1:T(8,128)(2,1)}, bf16[1024,1,1,512]{0,3,2,1:T(8,128)(2,1)S(1)}, u32[]{:S(2)}) copy-start(bf16[1024,1,1,512]{0,3,2,1:T(8,128)(2,1)S(1)} %copy.139) | copy-start | bytes 3145732
  71.1 25.9 %all-to-all-start.1 = ((bf16[2,2,32768]{2,1,0:T(2,128)(2,1)}), bf16[2,2,32768]{2,1,0:T(2,128)(2,1)S(1)}, u32[]{:S(2)}, u32[]{:S(2)}) async-start(bf16[2,2,32768]{2,1,0:T(2,128)(2,1)} %reshape.190), calls=%async_computation.1 | async-start | bytes 524288 | tf_op jit(solution)/shard_map/all_to_all | solution.py:91
  74.6 105.9 %reduce-scatter.3.cloned.1.call-start = ((), (), s32[]{:S(2)}) async-start(), calls=%async_computation.7 | async-start | bytes 5242880 | tf_op jit(solution)/shard_map/reduce_scatter | solution.py:155
  95.6 5.1 %copy-start.6 = (bf16[256,1024]{0,1:T(8,128)(2,1)}, bf16[256,1024]{0,1:T(8,128)(2,1)S(1)}, u32[]{:S(2)}) copy-start(bf16[256,1024]{0,1:T(8,128)(2,1)S(1)} %copy.145) | copy-start | bytes 1572868
  97.0 4.1 %copy-start.8 = (bf16[256,1024]{0,1:T(8,128)(2,1)}, bf16[256,1024]{0,1:T(8,128)(2,1)S(1)}, u32[]{:S(2)}) copy-start(bf16[256,1024]{0,1:T(8,128)(2,1)S(1)} %copy.143) | copy-start | bytes 1572868
  99.3 1.4 copy-start.4
  100.7 3.4 %copy-start.7 = (bf16[256,1024]{0,1:T(8,128)(2,1)S(1)}, bf16[256,1024]{0,1:T(8,128)(2,1)}, u32[]{:S(2)}) copy-start(bf16[256,1024]{0,1:T(8,128)(2,1)} %copy-done.6) | copy-start | bytes 1572868
  101.2 4.2 %copy-start.15 = (f32[1,128,1024]{1,2,0:T(8,128)S(1)}, f32[1,128,1024]{1,2,0:T(8,128)}, u32[]{:S(2)}) copy-start(f32[1,128,1024]{1,2,0:T(8,128)} %copy.147) | copy-start | bytes 1572868
  115.0 4.6 %copy-start.14 = (f32[256,8,64]{0,2,1:T(8,128)S(1)}, f32[256,8,64]{0,2,1:T(8,128)}, u32[]{:S(2)}) copy-start(f32[256,8,64]{0,2,1:T(8,128)} %get-tuple-element.42) | copy-start | bytes 1572868
  115.0 4.7 %copy-start = (bf16[8,256,1024]{2,1,0:T(8,128)(2,1)S(1)}, bf16[8,256,1024]{2,1,0:T(8,128)(2,1)}, u32[]{:S(2)}) copy-start(bf16[8,256,1024]{2,1,0:T(8,128)(2,1)} %exponential_convert_fusion) | copy-start | bytes 12582916
  115.1 4.7 %copy-start.3 = (bf16[1024,1,1,512]{0,3,2,1:T(8,128)(2,1)S(1)}, bf16[1024,1,1,512]{0,3,2,1:T(8,128)(2,1)}, u32[]{:S(2)}) copy-start(bf16[1024,1,1,512]{0,3,2,1:T(8,128)(2,1)} %copy-done.2) | copy-start | bytes 3145732
  119.7 3.9 %copy-start.12 = (bf16[256,1,1,512]{0,3,2,1:T(8,128)(2,1)S(1)}, bf16[256,1,1,512]{0,3,2,1:T(8,128)(2,1)}, u32[]{:S(2)}) copy-start(bf16[256,1,1,512]{0,3,2,1:T(8,128)(2,1)} %copy-done.11) | copy-start | bytes 786436
  121.7 2.0 copy-start.1
  136.4 5.1 %copy-start.10 = (bf16[1,128,1024]{1,2,0:T(8,128)(2,1)S(1)}, bf16[1,128,1024]{1,2,0:T(8,128)(2,1)}, u32[]{:S(2)}) copy-start(bf16[1,128,1024]{1,2,0:T(8,128)(2,1)} %copy-done.9) | copy-start | bytes 786436
  136.4 88.8 %reduce-scatter.5.cloned.1.call-start = ((), (), s32[]{:S(2)}) async-start(), calls=%async_computation.8 | async-start | bytes 2359296 | tf_op jit(solution)/shard_map/reduce_scatter | solution.py:115
  141.8 5.2 %copy-start.19 = (bf16[128,16,64]{0,2,1:T(8,128)(2,1)S(1)}, bf16[128,16,64]{0,2,1:T(8,128)(2,1)}, u32[]{:S(2)}) copy-start(bf16[128,16,64]{0,2,1:T(8,128)(2,1)} %get-tuple-element.47) | copy-start | bytes 786436
  143.2 4.7 %copy-start.16 = (f32[16,64,128]{2,1,0:T(8,128)S(1)}, f32[16,64,128]{2,1,0:T(8,128)}, u32[]{:S(2)}) copy-start(f32[16,64,128]{2,1,0:T(8,128)} %get-tuple-element.46) | copy-start | bytes 1572868
  143.2 4.9 %copy-start.5 = (f32[2,128,1,512]{1,3,0,2:T(8,128)S(1)}, f32[2,128,1,512]{1,3,0,2:T(8,128)}, u32[]{:S(2)}) copy-start(f32[2,128,1,512]{1,3,0,2:T(8,128)} %copy-done.4) | copy-start | bytes 1572868
  183.5 43.3 %all-to-all-start.3 = ((bf16[256,3,1,512]{3,1,2,0:T(4,128)(2,1)}), bf16[256,3,1,512]{3,1,2,0:T(4,128)(2,1)S(1)}, u32[]{:S(2)}, u32[]{:S(2)}) async-start(bf16[256,3,1,512]{3,1,2,0:T(4,128)(2,1)} %copy.154), calls=%async_computation.4 | async-start | bytes 2097152 | tf_op jit(solution)/shard_map/all_to_all | solution.py:171
Sparse Core Ops, SparseCore 0:
  26.0 17.3 all-gather.4
  45.5 16.9 all-gather.6
  136.6 43.8 reduce-scatter.2
  183.9 41.2 reduce-scatter.4
Sparse Core Ops, SparseCore 1:
  30.2 63.0 all-reduce.1
where the time goes:
time: 237 us; the launch traced here: 236 us
  waiting for transfers between devices  110 us (46%)
  local copies, waits for them, and re-layouts  33.4 us (14%)
  matrix products  25.9 us (11%)
  blocking collectives  22.5 us (9%)
  other arithmetic  20 us (8%)
  between operations  16.3 us (7%)
  starting transfers between devices  7.23 us (3%)
    reduce_scatter x1, waiting for transfers between devices, body(): lax.psum_scatter(thermal_sums(cross_probs, cross_dscores, cross_heads, up...  38.1 us
    reduce_scatter x1, waiting for transfers between devices, body(): lax.psum_scatter(jnp.concatenate([key_grad.reshape(lax.axis_size('seq') *...  27.6 us
    psum x1, waiting for transfers between devices, spread(): return lax.psum(block, axis)  18.7 us
    all_to_all x1, blocking collectives, body(): lax.all_to_all(packed, 'head', split_axis=2, concat_axis=0, tiled=True)  14.9 us
    all_gather x1, waiting for transfers between devices, body(): lax.all_gather(by_heads[:, 1, 0], 'seq', axis=0, tiled=True)  13.5 us
    all_gather x1, waiting for transfers between devices, body(): lax.all_gather(by_heads[:, 2, 0], 'seq', axis=0, tiled=True)  11.8 us
    unnamed x50, local copies, waits for them, and re-layouts  7.98 us
    all_to_all x1, blocking collectives, body(): lax.all_to_all(attended_grad.reshape(tokens_here, head_devices, local_wid...  7.56 us
  transfers between devices with their start and end apart: 7, of which 5 were waited for; matrix products, arithmetic and copies ran while one was open for 18% of the time, Pallas kernels for 0%

commit v1 on v0

--- a/solution.py
+++ b/solution.py
@@ -8,9 +8,15 @@
 HD = 64
 
 
+def gather_and_add(array, axis):
+    terms = lax.all_gather(array, axis, axis=0, tiled=False)
+    total = terms.sum(axis=0)
+    return total
+
+
 def spread(block, axis, owner):
     block = jnp.where(lax.axis_index(axis) == owner, block, jnp.zeros_like(block))
-    return lax.psum(block, axis)
+    return gather_and_add(block, axis)
 
 
 def log_total(scores):

time: 237 us -> 266 us (1.12)
  waiting for transfers between devices: 110 us -> 140 us
  other arithmetic: 20 us -> 23.8 us
    all_gather x0 -> x1, waiting for transfers between devices: none -> 33.4 us  [gather_and_add(): terms = lax.all_gather(array, axis, axis=0, tiled=False)]
    psum x1 -> x0, waiting for transfers between devices: 18.7 us -> none  [spread(): return lax.psum(block, axis)]
    all_to_all x1, waiting for transfers between devices: 0.01 us -> 7.53 us  [body(): lax.all_to_all(attended_heads.reshape(row_count, 1, local_width), 'head',...]
    all_gather x1, waiting for transfers between devices: 11.8 us -> 17.4 us  [body(): lax.all_gather(by_heads[:, 2, 0], 'seq', axis=0, tiled=True)]
    reduce_sum x0 -> x1, other arithmetic: none -> 5.21 us  [gather_and_add(): total = terms.sum(axis=0)]
    unnamed x50 -> x54, local copies, waits for them, and re-layouts: 7.98 us -> 9.2 us
  transfers between devices with their start and end apart: 7 -> 7, of which waited for: 5 -> 6; matrix products, arithmetic and copies ran while one was open for 18% -> 14% of each run, Pallas kernels for 0% -> 0%
where the time goes in v1:
time: 266 us; the launch traced here: 265 us
  waiting for transfers between devices  140 us (53%)
  local copies, waits for them, and re-layouts  32.5 us (12%)
  other arithmetic  23.8 us (9%)
  matrix products  23.3 us (9%)
  blocking collectives  23.1 us (9%)
  between operations  14.9 us (6%)
  starting transfers between devices  7.63 us (3%)
    reduce_scatter x1, waiting for transfers between devices, body(): lax.psum_scatter(thermal_sums(cross_probs, cross_dscores, cross_heads, up...  38.1 us
    all_gather x1, waiting for transfers between devices, gather_and_add(): terms = lax.all_gather(array, axis, axis=0, tiled=False)  33.4 us
    reduce_scatter x1, waiting for transfers between devices, body(): lax.psum_scatter(jnp.concatenate([key_grad.reshape(lax.axis_size('seq') *...  28.1 us
    all_gather x1, waiting for transfers between devices, body(): lax.all_gather(by_heads[:, 2, 0], 'seq', axis=0, tiled=True)  17.4 us
    all_to_all x1, blocking collectives, body(): lax.all_to_all(packed, 'head', split_axis=2, concat_axis=0, tiled=True)  14.8 us
    all_gather x1, waiting for transfers between devices, body(): lax.all_gather(by_heads[:, 1, 0], 'seq', axis=0, tiled=True)  14.6 us
    unnamed x54, local copies, waits for them, and re-layouts  9.2 us
    all_to_all x1, blocking collectives, body(): lax.all_to_all(attended_grad.reshape(tokens_here, head_devices, local_wid...  8.25 us
  transfers between devices with their start and end apart: 7, of which 6 were waited for; matrix products, arithmetic and copies ran while one was open for 14% of the time, Pallas kernels for 0%

profile of v1, /device:TPU:0, one launch (start us, length us, event | category | flops | bytes accessed | tf_op | source)
XLA Modules:
  0.0 265.1 jit_solution(3998797567958703219)
XLA Ops:
  7.2 1.6 copy.130
  9.1 14.8 %all_to_all.57 = bf16[128,3,2,512]{3,0,1,2:T(8,128)(2,1)S(1)} all-to-all(bf16[128,3,2,512]{3,0,1,2:T(8,128)(2,1)S(1)} %copy.131), channel_id=1, replica_groups=mesh['img'=4,'seq'=4,'head'=2] {'head'}, dimensions={2} | all-to-all | bytes 1572864 | tf_op jit(solution)/shard_map/all_to_all | solution.py:76
  24.0 0.8 fusion.9
  26.3 1.1 broadcast_select_fusion
  27.6 14.6 %all-gather.7.cloned.1.call-done = bf16[1024,1,1,512]{3,0,1,2:T(8,128)(2,1)} async-done(((bf16[256,1,1,512]{3,0,1,2:T(8,128)(2,1)}), bf16[1024,1,1,512]{3,0,1,2:T(8,128)(2,1)}) %all-gather.7.cloned.1.call-update) | async-done | bytes 1048592 | tf_op jit(solution)/shard_map/all_gather | solution.py:80
  42.2 1.5 copy.134
  43.7 17.4 %all-gather.9.cloned.1.call-done = bf16[1024,1,1,512]{3,0,1,2:T(8,128)(2,1)} async-done(((bf16[256,1,1,512]{3,0,1,2:T(8,128)(2,1)}), bf16[1024,1,1,512]{3,0,1,2:T(8,128)(2,1)}) %all-gather.9.cloned.1.call-update) | async-done | bytes 1048592 | tf_op jit(solution)/shard_map/all_gather | solution.py:81
  61.1 1.5 copy.135
  62.6 1.4 multiply_reduce_fusion
  63.9 1.7 exponential_reduce_fusion
  65.7 1.4 exponential_convert_fusion
  67.1 1.9 copy-done
  69.1 2.2 fusion.10
  71.8 0.8 reduce.2
  72.8 0.9 reshape.201
  73.6 3.4 %all-to-all-start.1 = ((bf16[2,2,32768]{2,1,0:T(2,128)(2,1)}), bf16[2,2,32768]{2,1,0:T(2,128)(2,1)S(1)}, u32[]{:S(2)}, u32[]{:S(2)}) async-start(bf16[2,2,32768]{2,1,0:T(2,128)(2,1)} %reshape.201), calls=%async_computation.1 | async-start | bytes 524288 | tf_op jit(solution)/shard_map/all_to_all | solution.py:97
  77.5 0.9 copy.143
  78.7 7.5 %all-to-all-done.1 = bf16[2,2,32768]{2,1,0:T(2,128)(2,1)S(1)} async-done(((bf16[2,2,32768]{2,1,0:T(2,128)(2,1)}), bf16[2,2,32768]{2,1,0:T(2,128)(2,1)S(1)}, u32[]{:S(2)}, u32[]{:S(2)}) %all-to-all-start.1) | async-done | bytes 262176 | tf_op jit(solution)/shard_map/all_to_all | solution.py:97
  86.8 33.4 %all-gather.11.cloned.1.call-done = bf16[8,1,256,2048]{3,2,1,0:T(8,128)(2,1)} async-done(((bf16[1,1,256,2048]{3,2,1,0:T(8,128)(2,1)}), bf16[8,1,256,2048]{3,2,1,0:T(8,128)(2,1)}) %all-gather.11.cloned.1.call-update) | async-done | bytes 8388624 | tf_op jit(solution)/shard_map/all_gather | solution.py:12
  120.2 5.2 %reduce_sum.49 = bf16[256,2048]{1,0:T(8,128)(2,1)S(1)} reduce(bf16[8,1,256,2048]{3,2,1,0:T(8,128)(2,1)} %all-gather.11.cloned.1.call-done, bf16[]{:T(256)} %constant.19.clone.1), dimensions={0,1}, to_apply=%region_2.3 | reduce | flops 3670016 | bytes 9437186 | tf_op jit(solution)/shard_map/reduce_sum | solution.py:13
  125.4 1.1 fusion.8
  126.5 1.2 copy.141
  129.8 1.3 fusion.3
  131.1 1.6 fusion.1
  132.7 1.2 bitcast_convert_fusion
  134.0 8.3 %all_to_all.58 = bf16[128,2,512]{0,2,1:T(8,128)(2,1)S(1)} all-to-all(bf16[128,2,512]{0,2,1:T(8,128)(2,1)S(1)} %add_convert_fusion), channel_id=1, replica_groups=mesh['img'=4,'seq'=4,'head'=2] {'head'}, dimensions={1} | all-to-all | bytes 524288 | tf_op jit(solution)/shard_map/all_to_all | solution.py:135
  142.3 1.0 copy.146
  143.2 1.1 reshape_reshape.3
  144.4 4.5 %fusion.11 = f32[8,64,1024]{2,1,0:T(8,128)} fusion(bf16[256,8,64]{0,2,1:T(8,128)(2,1)S(1)} %reshape_reshape.3, bf16[8,256,1024]{2,1,0:T(8,128)(2,1)} %copy-done), kind=kOutput, calls=%fused_computation.34 | convolution fusion | flops 268435456 | bytes 6553600 | tf_op jit(solution)/shard_map/hqk,qhd->khd/dot_general | solution.py:158
  149.1 1.9 multiply_convert_fusion
  151.0 1.9 copy-done.2
  152.9 2.2 fusion.12
  155.1 2.9 %copy.147 = f32[1024,512]{1,0:T(8,128)} copy(f32[1024,512]{0,1:T(8,128)} %bitcast.103) | data formatting | bytes 4194304 | tf_op jit(solution)/shard_map/reshape | solution.py:164
  158.1 2.9 %copy.148 = f32[1024,512]{1,0:T(8,128)} copy(f32[1024,512]{0,1:T(8,128)} %bitcast.102) | data formatting | bytes 4194304 | tf_op jit(solution)/shard_map/reshape | solution.py:165
  161.0 4.7 %pad_maximum_fusion = f32[1024,1024]{1,0:T(8,128)} fusion(f32[1024,512]{1,0:T(8,128)} %copy.148, f32[1024,512]{1,0:T(8,128)} %copy.147), kind=kLoop, calls=%fused_computation.4 | loop fusion | flops 1048576 | bytes 8388608 | tf_op jit(solution)/shard_map/concatenate | solution.py:162
  166.0 2.5 fusion.4
  168.5 2.6 copy.153
  171.4 1.4 copy.154
  172.8 3.8 %pad_maximum_fusion.1 = f32[256,2048]{1,0:T(8,128)} fusion(f32[256,1024]{1,0:T(8,128)} %copy.154, f32[256,1024]{1,0:T(8,128)} %copy.153), kind=kLoop, calls=%fused_computation.5 | loop fusion | flops 524288 | bytes 4194304 | tf_op jit(solution)/shard_map/concatenate | solution.py:62
  176.8 0.9 copy.156
  178.6 3.6 %convolution_convert_fusion = bf16[8,256,64]{1,2,0:T(8,128)(2,1)S(1)} fusion(bf16[8,256,1024]{2,1,0:T(8,128)(2,1)} %copy-done.2, bf16[1024,8,64]{0,2,1:T(8,128)(2,1)S(1)} %bitcast.99), kind=kOutput, calls=%fused_computation.13 | convolution fusion | flops 268566528 | bytes 5505024 | tf_op jit(solution)/shard_map/hqk,khd->qhd/dot_general | solution.py:151
  182.4 28.1 %reduce-scatter.3.cloned.1.call-done = f32[256,1024]{1,0:T(8,128)} async-done(((f32[1024,1024]{1,0:T(8,128)}), f32[256,1024]{1,0:T(8,128)}) %reduce-scatter.3.cloned.1.call-update) | async-done | bytes 1048592 | tf_op jit(solution)/shard_map/reduce_scatter | solution.py:161
  210.4 1.3 convert.23
  211.9 1.7 copy.150
  213.5 3.6 %all-to-all-start.3 = ((bf16[256,3,1,512]{3,1,2,0:T(4,128)(2,1)}), bf16[256,3,1,512]{3,1,2,0:T(4,128)(2,1)S(1)}, u32[]{:S(2)}, u32[]{:S(2)}) async-start(bf16[256,3,1,512]{3,1,2,0:T(4,128)(2,1)} %copy.150), calls=%async_computation.4 | async-start | bytes 2097152 | tf_op jit(solution)/shard_map/all_to_all | solution.py:177
  217.1 38.1 %reduce-scatter.5.cloned.1.call-done = f32[32,2048]{1,0:T(8,128)} async-done(((f32[256,2048]{1,0:T(8,128)}), f32[32,2048]{1,0:T(8,128)}) %reduce-scatter.5.cloned.1.call-update) | async-done | bytes 262160 | tf_op jit(solution)/shard_map/reduce_scatter | solution.py:121
  255.2 1.6 convert_bitcast_fusion
  257.4 1.2 copy.155
  (81 shorter events, 7.9 us)
Async XLA Ops:
  7.2 19.2 %copy-start.19 = (bf16[1,1,256,2048]{3,2,1,0:T(8,128)(2,1)S(1)}, bf16[1,1,256,2048]{3,2,1,0:T(8,128)(2,1)}, u32[]{:S(2)}) copy-start(bf16[1,1,256,2048]{3,2,1,0:T(8,128)(2,1)} %param.7) | copy-start | bytes 3145732
  7.2 35.0 %all-gather.7.cloned.1.call-start = ((), (), s32[]{:S(2)}) async-start(), calls=%async_computation.8 | async-start | bytes 1310720 | tf_op jit(solution)/shard_map/all_gather | solution.py:80
  24.9 36.2 %all-gather.9.cloned.1.call-start = ((), (), s32[]{:S(2)}) async-start(), calls=%async_computation.9 | async-start | bytes 1310720 | tf_op jit(solution)/shard_map/all_gather | solution.py:81
  25.6 94.6 %all-gather.11.cloned.1.call-start = ((), (), s32[]{:S(2)}) async-start(), calls=%async_computation.10 | async-start | bytes 9437184 | tf_op jit(solution)/shard_map/all_gather | solution.py:12
  27.6 36.4 %copy-start.12 = (bf16[256,1,1,512]{0,3,2,1:T(8,128)(2,1)}, bf16[256,1,1,512]{0,3,2,1:T(8,128)(2,1)S(1)}, u32[]{:S(2)}) copy-start(bf16[256,1,1,512]{0,3,2,1:T(8,128)(2,1)S(1)} %copy.133) | copy-start | bytes 786436
  62.5 4.6 %copy-start.3 = (bf16[1024,1,1,512]{0,3,2,1:T(8,128)(2,1)}, bf16[1024,1,1,512]{0,3,2,1:T(8,128)(2,1)S(1)}, u32[]{:S(2)}) copy-start(bf16[1024,1,1,512]{0,3,2,1:T(8,128)(2,1)S(1)} %copy.135) | copy-start | bytes 3145732
  67.1 2.0 copy-start
  67.1 10.2 %copy-start.20 = (bf16[1,128,1024]{2,1,0:T(8,128)(2,1)S(1)}, bf16[1,128,1024]{2,1,0:T(8,128)(2,1)}, u32[]{:S(2)}) copy-start(bf16[1,128,1024]{2,1,0:T(8,128)(2,1)} %param.9) | copy-start | bytes 786436
  69.1 9.4 %copy-start.22 = (bf16[1,128,1024]{2,1,0:T(8,128)(2,1)S(1)}, bf16[1,128,1024]{2,1,0:T(8,128)(2,1)}, u32[]{:S(2)}) copy-start(bf16[1,128,1024]{2,1,0:T(8,128)(2,1)} %param.6) | copy-start | bytes 786436
  73.6 12.5 %all-to-all-start.1 = ((bf16[2,2,32768]{2,1,0:T(2,128)(2,1)}), bf16[2,2,32768]{2,1,0:T(2,128)(2,1)S(1)}, u32[]{:S(2)}, u32[]{:S(2)}) async-start(bf16[2,2,32768]{2,1,0:T(2,128)(2,1)} %reshape.201), calls=%async_computation.1 | async-start | bytes 524288 | tf_op jit(solution)/shard_map/all_to_all | solution.py:97
  77.1 133.3 %reduce-scatter.3.cloned.1.call-start = ((), (), s32[]{:S(2)}) async-start(), calls=%async_computation.6 | async-start | bytes 5242880 | tf_op jit(solution)/shard_map/reduce_scatter | solution.py:161
  77.5 53.6 %copy-start.10 = (bf16[1,128,1024]{1,2,0:T(8,128)(2,1)}, bf16[1,128,1024]{1,2,0:T(8,128)(2,1)S(1)}, u32[]{:S(2)}) copy-start(bf16[1,128,1024]{1,2,0:T(8,128)(2,1)S(1)} %copy.144) | copy-start | bytes 786436
  78.6 49.1 %copy-start.14 = (bf16[1,128,1024]{1,2,0:T(8,128)(2,1)}, bf16[1,128,1024]{1,2,0:T(8,128)(2,1)S(1)}, u32[]{:S(2)}) copy-start(bf16[1,128,1024]{1,2,0:T(8,128)(2,1)S(1)} %copy.140) | copy-start | bytes 786436
  86.8 40.9 %copy-start.5 = (f32[2,128,1,512]{1,3,0,2:T(8,128)}, f32[2,128,1,512]{1,3,0,2:T(8,128)S(1)}, u32[]{:S(2)}) copy-start(f32[2,128,1,512]{1,3,0,2:T(8,128)S(1)} %copy.137) | copy-start | bytes 1572868
  127.7 1.4 copy-start.7
  128.3 1.2 copy-start.18
  129.8 1.3 copy-start.9
  129.8 3.0 %copy-start.8 = (bf16[256,1024]{0,1:T(8,128)(2,1)S(1)}, bf16[256,1024]{0,1:T(8,128)(2,1)}, u32[]{:S(2)}) copy-start(bf16[256,1024]{0,1:T(8,128)(2,1)} %copy-done.7) | copy-start | bytes 1572868
  129.8 4.2 %copy-start.16 = (f32[1,128,1024]{1,2,0:T(8,128)S(1)}, f32[1,128,1024]{1,2,0:T(8,128)}, u32[]{:S(2)}) copy-start(f32[1,128,1024]{1,2,0:T(8,128)} %copy.143) | copy-start | bytes 1572868
  144.4 4.6 %copy-start.15 = (f32[256,8,64]{0,2,1:T(8,128)S(1)}, f32[256,8,64]{0,2,1:T(8,128)}, u32[]{:S(2)}) copy-start(f32[256,8,64]{0,2,1:T(8,128)} %get-tuple-element.42) | copy-start | bytes 1572868
  144.4 4.6 %copy-start.1 = (bf16[8,256,1024]{2,1,0:T(8,128)(2,1)S(1)}, bf16[8,256,1024]{2,1,0:T(8,128)(2,1)}, u32[]{:S(2)}) copy-start(bf16[8,256,1024]{2,1,0:T(8,128)(2,1)} %copy-done) | copy-start | bytes 12582916
  144.4 4.6 %copy-start.4 = (bf16[1024,1,1,512]{0,3,2,1:T(8,128)(2,1)S(1)}, bf16[1024,1,1,512]{0,3,2,1:T(8,128)(2,1)}, u32[]{:S(2)}) copy-start(bf16[1024,1,1,512]{0,3,2,1:T(8,128)(2,1)} %copy-done.3) | copy-start | bytes 3145732
  149.0 3.9 %copy-start.13 = (bf16[256,1,1,512]{0,3,2,1:T(8,128)(2,1)S(1)}, bf16[256,1,1,512]{0,3,2,1:T(8,128)(2,1)}, u32[]{:S(2)}) copy-start(bf16[256,1,1,512]{0,3,2,1:T(8,128)(2,1)} %copy-done.12) | copy-start | bytes 786436
  151.0 1.9 copy-start.2
  165.7 5.4 %copy-start.11 = (bf16[1,128,1024]{1,2,0:T(8,128)(2,1)S(1)}, bf16[1,128,1024]{1,2,0:T(8,128)(2,1)}, u32[]{:S(2)}) copy-start(bf16[1,128,1024]{1,2,0:T(8,128)(2,1)} %copy-done.10) | copy-start | bytes 786436
  165.8 89.5 %reduce-scatter.5.cloned.1.call-start = ((), (), s32[]{:S(2)}) async-start(), calls=%async_computation.7 | async-start | bytes 2359296 | tf_op jit(solution)/shard_map/reduce_scatter | solution.py:121
  171.4 5.2 %copy-start.6 = (f32[2,128,1,512]{1,3,0,2:T(8,128)S(1)}, f32[2,128,1,512]{1,3,0,2:T(8,128)}, u32[]{:S(2)}) copy-start(f32[2,128,1,512]{1,3,0,2:T(8,128)} %copy-done.5) | copy-start | bytes 1572868
  172.8 4.0 %copy-start.21 = (bf16[128,16,64]{0,2,1:T(8,128)(2,1)S(1)}, bf16[128,16,64]{0,2,1:T(8,128)(2,1)}, u32[]{:S(2)}) copy-start(bf16[128,16,64]{0,2,1:T(8,128)(2,1)} %get-tuple-element.47) | copy-start | bytes 786436
  172.8 4.9 %copy-start.17 = (f32[16,64,128]{2,1,0:T(8,128)S(1)}, f32[16,64,128]{2,1,0:T(8,128)}, u32[]{:S(2)}) copy-start(f32[16,64,128]{2,1,0:T(8,128)} %get-tuple-element.46) | copy-start | bytes 1572868
  213.5 43.3 %all-to-all-start.3 = ((bf16[256,3,1,512]{3,1,2,0:T(4,128)(2,1)}), bf16[256,3,1,512]{3,1,2,0:T(4,128)(2,1)S(1)}, u32[]{:S(2)}, u32[]{:S(2)}) async-start(bf16[256,3,1,512]{3,1,2,0:T(4,128)(2,1)} %copy.150), calls=%async_computation.4 | async-start | bytes 2097152 | tf_op jit(solution)/shard_map/all_to_all | solution.py:177
Sparse Core Ops, SparseCore 0:
  25.0 17.1 all-gather.6
  44.3 16.7 all-gather.8
  63.0 57.1 all-gather.10
  165.9 44.4 reduce-scatter.2
  213.9 41.2 reduce-scatter.4
